TPU v7x, 128 devices: a whole 4x4x4 slice. The times are simulated.
128 devices in a mesh: req: 16 (over z, y), kv: 8 (over x, core).
Axes of the slice: x: 4, y: 4, z: 4, core: 2. Of those that a mesh axis runs over, the one named last changes fastest.
Arguments:
- hidden_in: bfloat16 [16384, 2048], P(('req', 'kv')), may hold values from -6 to 6
- slot_tokens: int32 [16384], replicated, may hold values from 0 to 16383, as said below
- cache_len: int32 [128], P('req'), may hold values from 1 to 2048, 65536 in all
- prefill_start: int32 [16], P('req'), may hold values from 0 to 2048
- key_cache: bfloat16 [128, 2048, 1024], P('req', None, 'kv')
- value_cache: bfloat16 [128, 2048, 1024], P('req', None, 'kv'), may hold values from -18 to 18
- key_prefix: bfloat16 [16, 2048, 1024], P('req', None, 'kv')
- value_prefix: bfloat16 [16, 2048, 1024], P('req', None, 'kv'), may hold values from -18 to 18
- attn_gain: float32 [2048], replicated, may hold values from 0.25 to 1.75
- q_proj: bfloat16 [2048, 2048], P(None, 'kv'), may hold values from -0.125 to 0.125
- k_proj: bfloat16 [2048, 1024], P(None, 'kv'), may hold values from -0.125 to 0.125
- v_proj: bfloat16 [2048, 1024], P(None, 'kv'), may hold values from -0.125 to 0.125
- q_gain: float32 [128], replicated, may hold values from 0.25 to 1.75
- k_gain: float32 [128], replicated, may hold values from 0.25 to 1.75
- o_proj: bfloat16 [2048, 2048], P('kv'), may hold values from -0.125 to 0.125
- ffn_gain: float32 [2048], replicated, may hold values from 0.25 to 1.75
- w_gate: bfloat16 [2048, 6144], P(None, 'req'), may hold values from -0.125 to 0.125
- w_up: bfloat16 [2048, 6144], P(None, 'req'), may hold values from -0.125 to 0.125
- w_down: bfloat16 [6144, 2048], P('req'), may hold values from -0.078125 to 0.078125
- final_gain: float32 [2048], replicated, may hold values from 0.25 to 1.75
- lm_head: bfloat16 [2048, 151936], P(None, ('req', 'kv')), may hold values from -0.375 to 0.375
Outputs:
- layer_out: bfloat16 [16384, 2048], P(('req', 'kv'))
- max_logit: float32 [144], replicated
Inputs may be any that keep to these rules, and one draw needn't show every extreme that they name: slot_tokens is a permutation of the batch's tokens; each device's 128 consecutive slots take exactly 1 token from each device's 128 consecutive batch tokens.
All inputs are finite; a program needn't handle non-finite values. No bound on the sum of `cache_len` on one device may be relied on, other than what follows from the above.
Results may differ from a plain program's by a relative error of at most 0.0085.
The roundings to bfloat16 on the way count: a program that leaves them out, or rounds other values in their place, can miss the bound.
Values may be sent and summed in bfloat16 or wider, within the bound.
A program may use at most 128 MiB of HBM per device.

v0:
```python
import jax
import jax.numpy as jnp
from jax import lax
from jax.sharding import PartitionSpec as P

EPS = 1e-06
NEG = -1e30


def spread(value, axis, root):
    mine = lax.axis_index(axis) == root
    return lax.psum(jnp.where(mine, value, jnp.zeros_like(value)), axis)


def norm_rows(values, gain_vec):
    wide = values.astype(jnp.float32)
    return wide * lax.rsqrt(jnp.mean(wide * wide, axis=-1, keepdims=True) + EPS) * gain_vec


def rotate(values, places):
    half_dim = values.shape[-1] // 2
    freqs = 1000000.0 ** (-(jnp.arange(half_dim, dtype=jnp.float32) * 2.0 / values.shape[-1]))
    angles = places[:, None] * freqs[None, :]
    cosine = jnp.cos(angles)[:, None, :]
    sine = jnp.sin(angles)[:, None, :]
    first_half = values[..., :half_dim]
    second_half = values[..., half_dim:]
    return jnp.concatenate(
        [first_half * cosine - second_half * sine, second_half * cosine + first_half * sine],
        axis=-1,
    )


def prefill_full(q_heads, key_old, value_old, key_new, value_new, start_at):
    old_len = key_old.shape[0]
    fresh_rows = q_heads.shape[0]
    factor = q_heads.shape[-1] ** (-0.5)
    all_keys = jnp.concatenate([key_old, key_new], axis=0)
    all_values = jnp.concatenate([value_old, value_new], axis=0)
    scores = (
        jnp.einsum("cgd,kd->gck", q_heads, all_keys, preferred_element_type=jnp.float32) * factor
    )
    key_index = jnp.arange(old_len + fresh_rows, dtype=jnp.int32)[None, :]
    row_index = jnp.arange(fresh_rows, dtype=jnp.int32)[:, None]
    allowed = jnp.where(key_index < old_len, key_index < start_at, key_index - old_len <= row_index)
    scores = jnp.where(allowed[None], scores, NEG)
    row_peak = jnp.max(scores, axis=-1, keepdims=True)
    expd = jnp.exp(scores - row_peak)
    weights = (expd / jnp.sum(expd, axis=-1, keepdims=True)).astype(jnp.bfloat16)
    return jnp.einsum(
        "gck,kd->cgd", weights, all_values, preferred_element_type=jnp.float32
    ).astype(jnp.bfloat16)


def decode_attend(q_heads, key_old, value_old, key_self, value_self, lengths):
    factor = q_heads.shape[-1] ** (-0.5)
    past = jnp.einsum("bgd,bld->bgl", q_heads, key_old, preferred_element_type=jnp.float32) * factor
    slot_index = jnp.arange(key_old.shape[1], dtype=jnp.int32)
    past = jnp.where(slot_index[None, None, :] < lengths[:, None, None], past, NEG)
    own_score = (
        jnp.einsum("bgd,bd->bg", q_heads, key_self, preferred_element_type=jnp.float32) * factor
    )
    row_peak = jnp.maximum(jnp.max(past, axis=-1), own_score)
    past_exp = jnp.exp(past - row_peak[..., None])
    own_exp = jnp.exp(own_score - row_peak)
    row_total = jnp.sum(past_exp, axis=-1) + own_exp
    past_w = (past_exp / row_total[..., None]).astype(jnp.bfloat16)
    own_w = (own_exp / row_total).astype(jnp.bfloat16)
    summed = jnp.einsum("bgl,bld->bgd", past_w, value_old, preferred_element_type=jnp.float32)
    summed = (
        summed + own_w.astype(jnp.float32)[..., None] * value_self.astype(jnp.float32)[:, None, :]
    )
    return summed.astype(jnp.bfloat16)


def regroup(rows_in):
    return lax.all_to_all(rows_in, ("req", "kv"), split_axis=0, concat_axis=0, tiled=True)


def shards(
    hidden_in,
    slot_tokens,
    cache_len,
    prefill_start,
    key_cache,
    value_cache,
    key_prefix,
    value_prefix,
    attn_gain,
    q_proj,
    k_proj,
    v_proj,
    q_gain,
    k_gain,
    o_proj,
    ffn_gain,
    w_gate,
    w_up,
    w_down,
    final_gain,
    lm_head,
):
    req_count = lax.axis_size("req")
    kv_count = lax.axis_size("kv")
    devices = req_count * kv_count
    rows_dev = hidden_in.shape[0]
    kv_index = lax.axis_index("kv")
    self_index = lax.axis_index("req") * kv_count + kv_index
    slot_table = slot_tokens.reshape(devices, rows_dev)
    from_self = slot_table // rows_dev == self_index
    send_rows = jnp.sum(jnp.where(from_self, slot_table - self_index * rows_dev, 0), axis=1)
    slot_place = lax.dynamic_index_in_dim(slot_table, self_index, 0, keepdims=False) // rows_dev
    arrived = regroup(hidden_in[send_rows])
    owner_rows = arrived[slot_place]
    rows_all = lax.all_gather(owner_rows, "kv", axis=0, tiled=True)
    normed = norm_rows(rows_all, attn_gain).astype(jnp.bfloat16)
    o_full = lax.all_gather(o_proj, "kv", axis=0, tiled=True)
    ff_dev = w_gate.shape[1]
    ff_piece = ff_dev // kv_count
    gate_w = lax.all_gather(
        lax.dynamic_slice_in_dim(w_gate, kv_index * ff_piece, ff_piece, axis=1),
        "req",
        axis=1,
        tiled=True,
    )
    up_w = lax.all_gather(
        lax.dynamic_slice_in_dim(w_up, kv_index * ff_piece, ff_piece, axis=1),
        "req",
        axis=1,
        tiled=True,
    )
    down_w = lax.all_gather(
        lax.dynamic_slice_in_dim(w_down, kv_index * ff_piece, ff_piece, axis=0),
        "req",
        axis=0,
        tiled=True,
    )
    q_cols = q_proj.shape[1]
    kv_cols = k_proj.shape[1]
    projected = jnp.concatenate(
        [
            jnp.dot(normed, q_proj, preferred_element_type=jnp.float32),
            jnp.dot(normed, k_proj, preferred_element_type=jnp.float32),
            jnp.dot(normed, v_proj, preferred_element_type=jnp.float32),
        ],
        axis=1,
    )
    tok_req = projected.shape[0]
    head_dim = q_gain.shape[0]
    dec_count = cache_len.shape[0]
    fresh_count = tok_req - dec_count
    q_raw = projected[:, :q_cols].reshape(tok_req, q_cols // head_dim, head_dim)
    k_raw = projected[:, q_cols : q_cols + kv_cols].reshape(tok_req, kv_cols // head_dim, head_dim)
    v_new = (
        projected[:, q_cols + kv_cols :]
        .astype(jnp.bfloat16)
        .reshape(tok_req, kv_cols // head_dim, head_dim)
    )
    places = jnp.concatenate(
        [prefill_start[0] + jnp.arange(fresh_count, dtype=jnp.int32), cache_len]
    ).astype(jnp.float32)
    queries = rotate(norm_rows(q_raw, q_gain), places).astype(jnp.bfloat16)
    keys_new = rotate(norm_rows(k_raw, k_gain), places).astype(jnp.bfloat16)
    pre_out = prefill_full(
        queries[:fresh_count],
        key_prefix[0, :, 0:head_dim],
        value_prefix[0, :, 0:head_dim],
        keys_new[:fresh_count, 0],
        v_new[:fresh_count, 0],
        prefill_start[0],
    )
    dec_out = decode_attend(
        queries[fresh_count:],
        key_cache,
        value_cache,
        keys_new[fresh_count:, 0],
        v_new[fresh_count:, 0],
        cache_len,
    )
    pieces = jnp.concatenate([pre_out, dec_out], axis=0)
    pieces, gate_w, up_w, down_w = lax.optimization_barrier((pieces, gate_w, up_w, down_w))
    attended = lax.all_gather(pieces.reshape(tok_req, q_cols), "kv", axis=1, tiled=True)
    resid = (
        rows_all.astype(jnp.float32) + jnp.dot(attended, o_full, preferred_element_type=jnp.float32)
    ).astype(jnp.bfloat16)
    ffn_in = norm_rows(resid, ffn_gain).astype(jnp.bfloat16)
    gate_part = jnp.dot(ffn_in, gate_w, preferred_element_type=jnp.float32)
    up_part = jnp.dot(ffn_in, up_w, preferred_element_type=jnp.float32)
    hidden_act = (jax.nn.silu(gate_part) * up_part).astype(jnp.bfloat16)
    down_part = jnp.dot(hidden_act, down_w, preferred_element_type=jnp.float32)
    ffn_part = lax.psum_scatter(down_part, "kv", scatter_dimension=0, tiled=True)
    mine = lax.dynamic_slice_in_dim(resid, kv_index * rows_dev, rows_dev, axis=0)
    out_rows = (mine.astype(jnp.float32) + ffn_part).astype(jnp.bfloat16)
    going_back = jnp.zeros_like(out_rows).at[slot_place].set(out_rows)
    returned = regroup(going_back)
    layer_out = jnp.zeros_like(hidden_in).at[send_rows].set(returned)
    tail_sum = lax.psum(down_part[fresh_count - 1 :], "kv")
    tail_out = (resid[fresh_count - 1 :].astype(jnp.float32) + tail_sum).astype(jnp.bfloat16)
    tail_rows = norm_rows(tail_out, final_gain).astype(jnp.bfloat16)
    local_peaks = jnp.max(
        jnp.dot(
            lax.all_gather(tail_rows, "req", axis=0, tiled=True),
            lm_head,
            preferred_element_type=jnp.float32,
        ),
        axis=1,
    )
    max_logit = lax.pmax(local_peaks, ("req", "kv"))
    return (layer_out, max_logit)


def solution(mesh):
    placed = (
        P(("req", "kv"), None),
        P(),
        P("req"),
        P("req"),
        P("req", None, "kv"),
        P("req", None, "kv"),
        P("req", None, "kv"),
        P("req", None, "kv"),
        P(),
        P(None, "kv"),
        P(None, "kv"),
        P(None, "kv"),
        P(),
        P(),
        P("kv", None),
        P(),
        P(None, "req"),
        P(None, "req"),
        P("req", None),
        P(),
        P(None, ("req", "kv")),
    )
    return jax.shard_map(
        shards, mesh=mesh, in_specs=placed, out_specs=(P(("req", "kv"), None), P()), check_vma=False
    )
```

profile of v0, /device:TPU:1, one launch (start us, length us, event | category | flops | bytes accessed | tf_op | source)
XLA Modules:
  0.0 573.7 jit_solution(5138658079195809557)
XLA Ops:
  8.3 2.6 gather_fusion
  13.5 11.5 %all-to-all-start = ((bf16[128,2,1024]{2,1,0:T(2,128)(2,1)}), bf16[128,2,1024]{2,1,0:T(2,128)(2,1)S(1)}, u32[]{:S(2)}, u32[]{:S(2)}) async-start(bf16[128,2,1024]{2,1,0:T(2,128)(2,1)} %reshape.450), calls=%async_computation | async-start | bytes 1048576 | tf_op jit(solution)/shard_map/all_to_all | solution.py:77
  25.8 13.0 %all-to-all-done = bf16[128,2,1024]{2,1,0:T(2,128)(2,1)S(1)} async-done(((bf16[128,2,1024]{2,1,0:T(2,128)(2,1)}), bf16[128,2,1024]{2,1,0:T(2,128)(2,1)S(1)}, u32[]{:S(2)}, u32[]{:S(2)}) %all-to-all-start) | async-done | bytes 524320 | tf_op jit(solution)/shard_map/all_to_all | solution.py:77
  39.5 1.7 gather_fusion.1
  44.9 1.6 constant_dynamic-slice_fusion
  48.5 1.9 multiply_cosine_fusion
  50.5 4.0 fusion.4
  54.5 15.7 %all-gather.19.cloned.1.call-done = bf16[1024,2048]{1,0:T(8,128)(2,1)} async-done(((bf16[128,2048]{1,0:T(8,128)(2,1)}), bf16[1024,2048]{1,0:T(8,128)(2,1)}) %all-gather.19.cloned.1.call-update) | async-done | bytes 4194320 | tf_op jit(solution)/shard_map/all_gather | solution.py:115
  70.1 3.2 fusion.10
  74.8 2.3 multiply_reduce_fusion
  77.1 1.6 copy.48
  78.7 3.7 multiply_reduce_fusion.1
  88.2 3.6 convolution_convert_fusion
  92.6 15.9 %fusion.78 = (f32[2,1016]{1,0:T(2,128)S(1)}, f32[2,1016,3064]{2,1,0:T(8,128)}) fusion(pred[1016,3064]{1,0:T(8,128)(4,1)} %fusion.4, bf16[1016,128]{1,0:T(8,128)(2,1)S(1)} %copy.47, bf16[2048,128]{1,0:T(8,128)(2,1)S(1)} %bitcast.93, bf16[1024,2,64]{2,0,1:T(8,128)(2,1)S(1)} %get-tuple-element.10, bf16[1024,2,64]{2,0,1:T(8,128)(2,1)S(1)} %get-tuple-element.11), kind=kOutput, calls=%fused_computation.144 | convolution fusion | flops 1621384704 | bytes 29334016 | tf_op jit(solution)/shard_map/sub | solution.py:48
  108.5 12.0 %fusion.18 = bf16[1016,2,128]{2,0,1:T(8,128)(2,1)S(1)} fusion(f32[2,1016,3064]{2,1,0:T(8,128)} %get-tuple-element.25, f32[2,1016]{1,0:T(2,128)S(1)} %get-tuple-element.24, bf16[1016,128]{1,0:T(8,128)(2,1)S(1)} %slice.54, bf16[2048,128]{1,0:T(8,128)(2,1)S(1)} %bitcast.94), kind=kOutput, calls=%fused_computation.32 | convolution fusion | flops 1608149248 | bytes 26216896 | tf_op jit(solution)/shard_map/gck,kd->cgd/dot_general | solution.py:50
  120.6 48.2 %all-gather.11.cloned.1.call-done = bf16[2048,768]{0,1:T(8,128)(2,1)} async-done(((bf16[2048,48]{0,1:T(8,128)(2,1)}), bf16[2048,768]{0,1:T(8,128)(2,1)}) %all-gather.11.cloned.1.call-update) | async-done | bytes 3145744 | tf_op jit(solution)/shard_map/all_gather | solution.py:126
  168.8 48.9 %all-gather.13.cloned.1.call-done = bf16[768,2048]{1,0:T(8,128)(2,1)} async-done(((bf16[48,2048]{1,0:T(8,128)(2,1)}), bf16[768,2048]{1,0:T(8,128)(2,1)}) %all-gather.13.cloned.1.call-update) | async-done | bytes 3145744 | tf_op jit(solution)/shard_map/all_gather | solution.py:132
  218.8 49.7 %all-gather.17.cloned.1.call-done = bf16[2048,2048]{1,0:T(8,128)(2,1)} async-done(((bf16[256,2048]{1,0:T(8,128)(2,1)}), bf16[2048,2048]{1,0:T(8,128)(2,1)}) %all-gather.17.cloned.1.call-update) | async-done | bytes 8388624 | tf_op jit(solution)/shard_map/all_gather | solution.py:117
  268.5 34.4 %all-gather.15.cloned.1.call-done = bf16[1024,2048]{0,1:T(8,128)(2,1)} async-done(((bf16[1024,256]{0,1:T(8,128)(2,1)}), bf16[1024,2048]{0,1:T(8,128)(2,1)}) %all-gather.15.cloned.1.call-update) | async-done | bytes 4194320 | tf_op jit(solution)/shard_map/all_gather | solution.py:182
  302.9 14.2 %fusion.7 = (f32[1024]{0:T(1024)S(1)}, bf16[1024,2048]{1,0:T(8,128)(2,1)S(1)}) fusion(bf16[1024,2048]{0,1:T(8,128)(2,1)} %all-gather.15.cloned.1.call-done, bf16[2048,2048]{1,0:T(8,128)(2,1)} %all-gather.17.cloned.1.call-done, bf16[1024,2048]{1,0:T(8,128)(2,1)} %all-gather.19.cloned.1.call-done), kind=kOutput, calls=%fused_computation.20 | convolution fusion | flops 8602516480 | bytes 20975616 | tf_op jit(solution)/shard_map/dot_general | solution.py:184
  317.1 1.9 copy-done.7
  319.0 7.1 %fusion.20 = f32[1024,768]{1,0:T(8,128)} fusion(bf16[2048,768]{0,1:T(8,128)(2,1)} %all-gather.9.cloned.1.call-done, bf16[1024,2048]{1,0:T(8,128)(2,1)S(1)} %get-tuple-element.27, f32[2048]{0:T(1024)S(1)} %copy-done.17, f32[1024]{0:T(1024)S(1)} %add_rsqrt_fusion.1), kind=kOutput, calls=%fused_computation.33 | convolution fusion | flops 3229614080 | bytes 10498048 | tf_op jit(solution)/shard_map/dot_general | solution.py:187
  326.2 14.1 %fusion.23 = f32[1024,2048]{1,0:T(8,128)} fusion(bf16[768,2048]{1,0:T(8,128)(2,1)} %all-gather.13.cloned.1.call-done, f32[1024,768]{1,0:T(8,128)} %fusion.20, bf16[2048,768]{0,1:T(8,128)(2,1)} %all-gather.11.cloned.1.call-done, bf16[1024,2048]{1,0:T(8,128)(2,1)} %copy-done.7, f32[2048]{0:T(1024)S(1)} %copy-done.17, f32[1024]{0:T(1024)S(1)} %add_rsqrt_fusion.1), kind=kOutput, calls=%fused_computation.34 | convolution fusion | flops 6455558144 | bytes 22032384 | tf_op jit(solution)/shard_map/dot_general | solution.py:190
  340.2 1.6 slice.65
  342.6 56.0 %all-reduce.2.cloned.1.call-done = f32[9,2048]{1,0:T(8,128)} async-done(((f32[9,2048]{1,0:T(8,128)}), f32[9,2048]{1,0:T(8,128)}) %all-reduce.2.cloned.1.call-update) | async-done | bytes 73744 | tf_op jit(solution)/shard_map/psum | solution.py:197
  400.6 53.5 %reduce-scatter.2.cloned.1.call-done = f32[128,2048]{1,0:T(8,128)} async-done(((f32[1024,2048]{1,0:T(8,128)}), f32[128,2048]{1,0:T(8,128)}) %reduce-scatter.2.cloned.1.call-update) | async-done | bytes 1048592 | tf_op jit(solution)/shard_map/reduce_scatter | solution.py:191
  454.1 2.6 scatter_custom_fusion
  458.9 8.4 %all-to-all-start.1 = ((bf16[128,2,1024]{2,1,0:T(2,128)(2,1)}), bf16[128,2,1024]{2,1,0:T(2,128)(2,1)S(1)}, u32[]{:S(2)}, u32[]{:S(2)}) async-start(bf16[128,2,1024]{2,1,0:T(2,128)(2,1)} %reshape.452), calls=%async_computation.2 | async-start | bytes 1048576 | tf_op jit(solution)/shard_map/all_to_all | solution.py:77
  467.3 22.4 %all-gather.1 = bf16[16,9,2048]{2,1,0:T(8,128)(2,1)S(1)} all-gather(bf16[1,9,2048]{2,1,0:T(8,128)(2,1)S(1)} %fusion.51), channel_id=1, replica_groups=mesh['req'=16,'kv'=8] {'req'}, dimensions={0}, use_global_device_ids=true | all-gather | bytes 626688 | tf_op jit(solution)/shard_map/all_gather | solution.py:202
  490.8 4.4 convolution_reduce_fusion
  495.2 68.5 %pmax.7 = f32[144]{0:T(256)} all-reduce(f32[144]{0:T(256)S(1)} %convolution_reduce_fusion), channel_id=1, replica_groups=mesh['req'=16,'kv'=8] {'req','kv'}, use_global_device_ids=true, to_apply=%region_15.16 | all-reduce | flops 144 | bytes 1152 | tf_op jit(solution)/shard_map/pmax | solution.py:208
  564.2 2.4 scatter_custom_fusion.1
  (106 shorter events, 25.7 us)
Async XLA Ops:
  7.2 34.2 %copy-start = (bf16[2048,384]{1,0:T(8,128)(2,1)S(1)}, bf16[2048,384]{1,0:T(8,128)(2,1)}, u32[]{:S(2)}) copy-start(bf16[2048,384]{1,0:T(8,128)(2,1)} %param.37) | copy-start | bytes 4718596
  13.5 25.2 %all-to-all-start = ((bf16[128,2,1024]{2,1,0:T(2,128)(2,1)}), bf16[128,2,1024]{2,1,0:T(2,128)(2,1)S(1)}, u32[]{:S(2)}, u32[]{:S(2)}) async-start(bf16[128,2,1024]{2,1,0:T(2,128)(2,1)} %reshape.450), calls=%async_computation | async-start | bytes 1048576 | tf_op jit(solution)/shard_map/all_to_all | solution.py:77
  25.0 45.1 %all-gather.19.cloned.1.call-start = ((), (), s32[]{:S(2)}) async-start(), calls=%async_computation.10 | async-start | bytes 4718592 | tf_op jit(solution)/shard_map/all_gather | solution.py:115
  41.2 7.1 %copy-start.10 = (s32[8]{0:T(128)S(1)}, s32[8]{0:T(128)}, u32[]{:S(2)}) copy-start(s32[8]{0:T(128)} %param.23) | copy-start | bytes 100
  41.3 79.3 %all-gather.9.cloned.1.call-start = ((), (), s32[]{:S(2)}) async-start(), calls=%async_computation.3 | async-start | bytes 3342336 | tf_op jit(solution)/shard_map/all_gather | solution.py:120
  42.5 126.3 %all-gather.11.cloned.1.call-start = ((), (), s32[]{:S(2)}) async-start(), calls=%async_computation.4 | async-start | bytes 3342336 | tf_op jit(solution)/shard_map/all_gather | solution.py:126
  44.8 172.8 %all-gather.13.cloned.1.call-start = ((), (), s32[]{:S(2)}) async-start(), calls=%async_computation.5 | async-start | bytes 3342336 | tf_op jit(solution)/shard_map/all_gather | solution.py:132
  46.5 221.9 %all-gather.17.cloned.1.call-start = ((), (), s32[]{:S(2)}) async-start(), calls=%async_computation.7 | async-start | bytes 9437184 | tf_op jit(solution)/shard_map/all_gather | solution.py:117
  47.1 255.8 %all-gather.15.cloned.1.call-start = ((), (), s32[]{:S(2)}) async-start(), calls=%async_computation.6 | async-start | bytes 4718592 | tf_op jit(solution)/shard_map/all_gather | solution.py:182
  48.5 24.9 %copy-start.8 = (f32[2048]{0:T(1024)S(1)}, f32[2048]{0:T(1024)}, u32[]{:S(2)}) copy-start(f32[2048]{0:T(1024)} %param.29) | copy-start | bytes 24580
  70.1 3.4 copy-start.2
  73.6 1.2 copy-start.13
  74.8 2.3 copy-start.3
  74.8 3.9 copy-start.6
  77.1 5.3 copy-start.11
  78.7 5.4 copy-start.12
  84.1 2.2 copy-start.4
  84.9 3.2 copy-start.14
  88.1 3.7 copy-start.5
  88.2 4.5 copy-start.15
  92.6 15.9 %copy-start.16 = (bf16[1,2048,128]{2,1,0:T(8,128)(2,1)S(1)}, bf16[1,2048,128]{2,1,0:T(8,128)(2,1)}, u32[]{:S(2)}) copy-start(bf16[1,2048,128]{2,1,0:T(8,128)(2,1)} %param.28) | copy-start | bytes 1572868
  218.7 100.3 %copy-start.17 = (f32[2048]{0:T(1024)S(1)}, f32[2048]{0:T(1024)}, u32[]{:S(2)}) copy-start(f32[2048]{0:T(1024)} %param.36) | copy-start | bytes 24580
  218.7 179.8 %all-reduce.2.cloned.1.call-start = ((), (), s32[]{:S(2)}) async-start(), calls=%async_computation.9 | async-start | bytes 262144 | tf_op jit(solution)/shard_map/psum | solution.py:197
  317.1 1.9 copy-start.7
  341.8 57.8 %copy-start.9 = (f32[2048]{0:T(1024)S(1)}, f32[2048]{0:T(1024)}, u32[]{:S(2)}) copy-start(f32[2048]{0:T(1024)} %param.40) | copy-start | bytes 24580
  341.8 112.3 %reduce-scatter.2.cloned.1.call-start = ((), (), s32[]{:S(2)}) async-start(), calls=%async_computation.8 | async-start | bytes 9437184 | tf_op jit(solution)/shard_map/reduce_scatter | solution.py:191
  458.9 104.8 %all-to-all-start.1 = ((bf16[128,2,1024]{2,1,0:T(2,128)(2,1)}), bf16[128,2,1024]{2,1,0:T(2,128)(2,1)S(1)}, u32[]{:S(2)}, u32[]{:S(2)}) async-start(bf16[128,2,1024]{2,1,0:T(2,128)(2,1)} %reshape.452), calls=%async_computation.2 | async-start | bytes 1048576 | tf_op jit(solution)/shard_map/all_to_all | solution.py:77
  489.7 76.9 %copy-start.1 = (bf16[2048,384]{1,0:T(8,128)(2,1)S(1)}, bf16[2048,384]{1,0:T(8,128)(2,1)}, u32[]{:S(2)}) copy-start(bf16[2048,384]{1,0:T(8,128)(2,1)} %param.37) | copy-start | bytes 4718596
Sparse Core Ops, SparseCore 0:
  41.4 28.7 all-gather.18
  72.3 47.3 all-gather.8
  121.8 46.8 all-gather.10
  170.8 46.8 all-gather.12
  219.2 49.1 all-gather.16
  270.6 32.2 all-gather.14
  341.9 56.5 all-reduce.1
  401.1 52.9 reduce-scatter.1
where the time goes:
time: 578 us; the launch traced here: 574 us
  waiting for transfers between devices  321 us (56%)
  blocking collectives  90.9 us (16%)
  matrix products  79.3 us (14%)
  local copies, waits for them, and re-layouts  24.9 us (4%)
  other arithmetic  21.6 us (4%)
  starting transfers between devices  20.8 us (4%)
  between operations  15.5 us (3%)
    pmax x1, blocking collectives, shards(): max_logit = lax.pmax(local_peaks, ('req', 'kv'))  68.5 us
    psum x1, waiting for transfers between devices, shards(): tail_sum = lax.psum(down_part[fresh_count - 1:], 'kv')  56 us
    reduce_scatter x1, waiting for transfers between devices, shards(): lax.psum_scatter(down_part, 'kv', scatter_dimension=0, tiled=True)  53.5 us
    all_gather x1, waiting for transfers between devices, shards(): o_full = lax.all_gather(o_proj, 'kv', axis=0, tiled=True)  49.7 us
    all_gather x1, waiting for transfers between devices, shards(): lax.all_gather(lax.dynamic_slice_in_dim(w_down, kv_index * ff_piece, ff_p...  48.9 us
    all_gather x1, waiting for transfers between devices, shards(): lax.all_gather(lax.dynamic_slice_in_dim(w_up, kv_index * ff_piece, ff_pie...  48.2 us
    all_gather x1, waiting for transfers between devices, shards(): lax.all_gather(pieces.reshape(tok_req, q_cols), 'kv', axis=1, tiled=True)  34.4 us
    all_gather x1, blocking collectives, shards(): lax.all_gather(tail_rows, 'req', axis=0, tiled=True)  22.4 us
  transfers between devices with their start and end apart: 10, of which 8 were waited for; matrix products, arithmetic and copies ran while one was open for 12% of the time, Pallas kernels for 0%

commit v1 on v0

--- a/solution.py
+++ b/solution.py
@@ -112,7 +112,12 @@
     slot_place = lax.dynamic_index_in_dim(slot_table, self_index, 0, keepdims=False) // rows_dev
     arrived = regroup(hidden_in[send_rows])
     owner_rows = arrived[slot_place]
-    rows_all = lax.all_gather(owner_rows, "kv", axis=0, tiled=True)
+    ring = [owner_rows]
+    for hop in range(7):
+        ring.append(lax.ppermute(ring[-1], "kv", [(dev, (dev + 1) % 8) for dev in range(8)]))
+    rows_all = jnp.roll(
+        jnp.concatenate(ring[::-1], axis=0), (lax.axis_index("kv") + 1) * ring[0].shape[0], axis=0
+    )
     normed = norm_rows(rows_all, attn_gain).astype(jnp.bfloat16)
     o_full = lax.all_gather(o_proj, "kv", axis=0, tiled=True)
     ff_dev = w_gate.shape[1]

time: 578 us -> 529 us (0.915)
  waiting for transfers between devices: 321 us -> 246 us
  starting transfers between devices: 20.8 us -> 35 us
  local copies, waits for them, and re-layouts: 24.9 us -> 30.7 us
    all_gather x1, waiting for transfers between devices: 48.9 us -> 0.02 us  [shards(): lax.all_gather(lax.dynamic_slice_in_dim(w_down, kv_index * ff_piece, ff_p...]
    all_gather x1, waiting for transfers between devices: 48.2 us -> 0.02 us  [shards(): lax.all_gather(lax.dynamic_slice_in_dim(w_up, kv_index * ff_piece, ff_pie...]
    ppermute x0 -> x7, waiting for transfers between devices: none -> 36.7 us  [shards(): lax.ppermute(ring[-1], 'kv', [(dev, (dev + 1) % 8) for dev in range(8)])]
    all_gather x1 -> x0, waiting for transfers between devices: 15.7 us -> none  [shards(): rows_all = lax.all_gather(owner_rows, 'kv', axis=0, tiled=True)]
    ppermute x0 -> x7, starting transfers between devices: none -> 14.8 us  [shards(): lax.ppermute(ring[-1], 'kv', [(dev, (dev + 1) % 8) for dev in range(8)])]
    unnamed x44 -> x57, local copies, waits for them, and re-layouts: 9.87 us -> 16.4 us
  transfers between devices with their start and end apart: 10 -> 16, of which waited for: 8 -> 12; matrix products, arithmetic and copies ran while one was open for 12% -> 16% of each run, Pallas kernels for 0% -> 0%
where the time goes in v1:
time: 529 us; the launch traced here: 523 us
  waiting for transfers between devices  246 us (47%)
  blocking collectives  90.9 us (17%)
  matrix products  84 us (16%)
  starting transfers between devices  35 us (7%)
  local copies, waits for them, and re-layouts  30.7 us (6%)
  other arithmetic  20.8 us (4%)
  between operations  15.6 us (3%)
    pmax x1, blocking collectives, shards(): max_logit = lax.pmax(local_peaks, ('req', 'kv'))  68.6 us
    psum x1, waiting for transfers between devices, shards(): tail_sum = lax.psum(down_part[fresh_count - 1:], 'kv')  56.3 us
    reduce_scatter x1, waiting for transfers between devices, shards(): lax.psum_scatter(down_part, 'kv', scatter_dimension=0, tiled=True)  53.4 us
    all_gather x1, waiting for transfers between devices, shards(): o_full = lax.all_gather(o_proj, 'kv', axis=0, tiled=True)  51.3 us
    ppermute x7, waiting for transfers between devices, shards(): lax.ppermute(ring[-1], 'kv', [(dev, (dev + 1) % 8) for dev in range(8)])  36.7 us
    all_gather x1, waiting for transfers between devices, shards(): lax.all_gather(pieces.reshape(tok_req, q_cols), 'kv', axis=1, tiled=True)  34 us
    all_gather x1, blocking collectives, shards(): lax.all_gather(tail_rows, 'req', axis=0, tiled=True)  22.4 us
    all_to_all x2, starting transfers between devices, regroup(): lax.all_to_all(rows_in, ('req', 'kv'), split_axis=0, concat_axis=0, tiled...  19.9 us
  transfers between devices with their start and end apart: 16, of which 12 were waited for; matrix products, arithmetic and copies ran while one was open for 16% of the time, Pallas kernels for 0%

profile of v1, /device:TPU:1, one launch (start us, length us, event | category | flops | bytes accessed | tf_op | source)
XLA Modules:
  0.0 523.0 jit_solution(8011846986419430282)
XLA Ops:
  13.1 2.6 gather_fusion
  18.3 11.5 %all-to-all-start = ((bf16[128,2,1024]{2,1,0:T(2,128)(2,1)}), bf16[128,2,1024]{2,1,0:T(2,128)(2,1)S(1)}, u32[]{:S(2)}, u32[]{:S(2)}) async-start(bf16[128,2,1024]{2,1,0:T(2,128)(2,1)} %reshape.449), calls=%async_computation | async-start | bytes 1048576 | tf_op jit(solution)/shard_map/all_to_all | solution.py:77
  30.6 13.0 %all-to-all-done = bf16[128,2,1024]{2,1,0:T(2,128)(2,1)S(1)} async-done(((bf16[128,2,1024]{2,1,0:T(2,128)(2,1)}), bf16[128,2,1024]{2,1,0:T(2,128)(2,1)S(1)}, u32[]{:S(2)}, u32[]{:S(2)}) %all-to-all-start) | async-done | bytes 524320 | tf_op jit(solution)/shard_map/all_to_all | solution.py:77
  46.3 6.1 %collective-permute-done = bf16[128,2048]{1,0:T(8,128)(2,1)S(1)} collective-permute-done((bf16[128,2048]{1,0:T(8,128)(2,1)S(1)}, bf16[128,2048]{1,0:T(8,128)(2,1)S(1)}, u32[]{:S(2)}, u32[]{:S(2)}) %collective-permute-start) | collective-permute-done | bytes 524320 | tf_op jit(solution)/shard_map/ppermute | solution.py:117
  52.4 2.5 collective-permute-start.1
  54.9 6.1 %collective-permute-done.1 = bf16[128,2048]{1,0:T(8,128)(2,1)S(1)} collective-permute-done((bf16[128,2048]{1,0:T(8,128)(2,1)S(1)}, bf16[128,2048]{1,0:T(8,128)(2,1)S(1)}, u32[]{:S(2)}, u32[]{:S(2)}) %collective-permute-start.1) | collective-permute-done | bytes 524320 | tf_op jit(solution)/shard_map/ppermute | solution.py:117
  61.1 2.5 collective-permute-start.2
  63.5 6.1 %collective-permute-done.2 = bf16[128,2048]{1,0:T(8,128)(2,1)S(1)} collective-permute-done((bf16[128,2048]{1,0:T(8,128)(2,1)S(1)}, bf16[128,2048]{1,0:T(8,128)(2,1)S(1)}, u32[]{:S(2)}, u32[]{:S(2)}) %collective-permute-start.2) | collective-permute-done | bytes 524320 | tf_op jit(solution)/shard_map/ppermute | solution.py:117
  74.5 3.8 collective-permute-done.3
  80.9 6.0 %collective-permute-done.4 = bf16[128,2048]{1,0:T(8,128)(2,1)S(1)} collective-permute-done((bf16[128,2048]{1,0:T(8,128)(2,1)S(1)}, bf16[128,2048]{1,0:T(8,128)(2,1)S(1)}, u32[]{:S(2)}, u32[]{:S(2)}) %collective-permute-start.4) | collective-permute-done | bytes 524320 | tf_op jit(solution)/shard_map/ppermute | solution.py:117
  89.4 4.0 fusion.4
  93.4 3.4 collective-permute-done.5
  98.1 3.6 multiply_cosine_fusion
  101.7 5.2 collective-permute-done.6
  119.7 3.7 multiply_reduce_fusion.1
  126.0 3.6 fusion.77
  130.2 3.6 convolution_convert_fusion
  133.8 2.9 fusion.48
  136.8 16.0 %fusion.78 = (f32[2,1016]{1,0:T(2,128)S(1)}, f32[2,1016,3064]{2,1,0:T(8,128)}) fusion(pred[1016,3064]{1,0:T(8,128)(4,1)} %fusion.4, bf16[1016,128]{1,0:T(8,128)(2,1)S(1)} %copy.47, bf16[2048,128]{1,0:T(8,128)(2,1)S(1)} %bitcast.93, bf16[1024,2,64]{2,0,1:T(8,128)(2,1)S(1)} %get-tuple-element.10, bf16[1024,2,64]{2,0,1:T(8,128)(2,1)S(1)} %get-tuple-element.11), kind=kOutput, calls=%fused_computation.160 | convolution fusion | flops 1621384704 | bytes 29334016 | tf_op jit(solution)/shard_map/sub | solution.py:48
  152.8 12.0 %fusion.18 = bf16[1016,2,128]{2,0,1:T(8,128)(2,1)S(1)} fusion(f32[2,1016,3064]{2,1,0:T(8,128)} %get-tuple-element.25, f32[2,1016]{1,0:T(2,128)S(1)} %get-tuple-element.24, bf16[1016,128]{1,0:T(8,128)(2,1)S(1)} %slice.54, bf16[2048,128]{1,0:T(8,128)(2,1)S(1)} %bitcast.94), kind=kOutput, calls=%fused_computation.32 | convolution fusion | flops 1608149248 | bytes 26216896 | tf_op jit(solution)/shard_map/gck,kd->cgd/dot_general | solution.py:50
  166.6 34.0 %all-gather.13.cloned.1.call-done = bf16[1024,2048]{0,1:T(8,128)(2,1)} async-done(((bf16[1024,256]{0,1:T(8,128)(2,1)}), bf16[1024,2048]{0,1:T(8,128)(2,1)}) %all-gather.13.cloned.1.call-update) | async-done | bytes 4194320 | tf_op jit(solution)/shard_map/all_gather | solution.py:187
  200.6 51.3 %all-gather.15.cloned.1.call-done = bf16[2048,2048]{1,0:T(8,128)(2,1)} async-done(((bf16[256,2048]{1,0:T(8,128)(2,1)}), bf16[2048,2048]{1,0:T(8,128)(2,1)}) %all-gather.15.cloned.1.call-update) | async-done | bytes 8388624 | tf_op jit(solution)/shard_map/all_gather | solution.py:122
  251.9 14.2 %fusion.7 = (f32[1024]{0:T(1024)S(1)}, bf16[1024,2048]{1,0:T(8,128)(2,1)S(1)}) fusion(bf16[1024,2048]{0,1:T(8,128)(2,1)} %all-gather.13.cloned.1.call-done, bf16[2048,2048]{1,0:T(8,128)(2,1)} %all-gather.15.cloned.1.call-done, bf16[2048,2048]{1,0:T(8,128)(2,1)} %copy-done.3, s32[]{:T(128)S(6)} %select_n.91), kind=kOutput, calls=%fused_computation.20 | convolution fusion | flops 8602516480 | bytes 20975620 | tf_op jit(solution)/shard_map/dot_general | solution.py:189
  268.0 7.1 %fusion.20 = f32[1024,768]{1,0:T(8,128)} fusion(bf16[2048,768]{0,1:T(8,128)(2,1)} %all-gather.7.cloned.1.call-done, bf16[1024,2048]{1,0:T(8,128)(2,1)S(1)} %get-tuple-element.27, f32[2048]{0:T(1024)S(1)} %copy-done.16, f32[1024]{0:T(1024)S(1)} %add_rsqrt_fusion.1), kind=kOutput, calls=%fused_computation.33 | convolution fusion | flops 3229614080 | bytes 10498048 | tf_op jit(solution)/shard_map/dot_general | solution.py:192
  275.2 14.1 %fusion.23 = f32[1024,2048]{1,0:T(8,128)} fusion(bf16[768,2048]{1,0:T(8,128)(2,1)} %all-gather.11.cloned.1.call-done, f32[1024,768]{1,0:T(8,128)} %fusion.20, bf16[2048,768]{0,1:T(8,128)(2,1)} %all-gather.9.cloned.1.call-done, bf16[1024,2048]{1,0:T(8,128)(2,1)} %copy-done.7, f32[2048]{0:T(1024)S(1)} %copy-done.16, f32[1024]{0:T(1024)S(1)} %add_rsqrt_fusion.1), kind=kOutput, calls=%fused_computation.34 | convolution fusion | flops 6455558144 | bytes 22032384 | tf_op jit(solution)/shard_map/dot_general | solution.py:195
  291.6 56.3 %all-reduce.2.cloned.1.call-done = f32[9,2048]{1,0:T(8,128)} async-done(((f32[9,2048]{1,0:T(8,128)}), f32[9,2048]{1,0:T(8,128)}) %all-reduce.2.cloned.1.call-update) | async-done | bytes 73744 | tf_op jit(solution)/shard_map/psum | solution.py:202
  350.0 53.4 %reduce-scatter.2.cloned.1.call-done = f32[128,2048]{1,0:T(8,128)} async-done(((f32[1024,2048]{1,0:T(8,128)}), f32[128,2048]{1,0:T(8,128)}) %reduce-scatter.2.cloned.1.call-update) | async-done | bytes 1048592 | tf_op jit(solution)/shard_map/reduce_scatter | solution.py:196
  403.4 2.6 scatter_custom_fusion
  408.2 8.4 %all-to-all-start.1 = ((bf16[128,2,1024]{2,1,0:T(2,128)(2,1)}), bf16[128,2,1024]{2,1,0:T(2,128)(2,1)S(1)}, u32[]{:S(2)}, u32[]{:S(2)}) async-start(bf16[128,2,1024]{2,1,0:T(2,128)(2,1)} %reshape.451), calls=%async_computation.2 | async-start | bytes 1048576 | tf_op jit(solution)/shard_map/all_to_all | solution.py:77
  416.6 22.4 %all-gather = bf16[16,9,2048]{2,1,0:T(8,128)(2,1)S(1)} all-gather(bf16[1,9,2048]{2,1,0:T(8,128)(2,1)S(1)} %fusion.51), channel_id=1, replica_groups=mesh['req'=16,'kv'=8] {'req'}, dimensions={0}, use_global_device_ids=true | all-gather | bytes 626688 | tf_op jit(solution)/shard_map/all_gather | solution.py:207
  440.1 4.4 convolution_reduce_fusion
  444.4 68.6 %pmax.7 = f32[144]{0:T(256)} all-reduce(f32[144]{0:T(256)S(1)} %convolution_reduce_fusion), channel_id=1, replica_groups=mesh['req'=16,'kv'=8] {'req','kv'}, use_global_device_ids=true, to_apply=%region_15.16 | all-reduce | flops 144 | bytes 1152 | tf_op jit(solution)/shard_map/pmax | solution.py:213
  (131 shorter events, 52.7 us)
Async XLA Ops:
  7.2 157.7 %all-gather.7.cloned.1.call-start = ((), (), s32[]{:S(2)}) async-start(), calls=%async_computation.3 | async-start | bytes 3342336 | tf_op jit(solution)/shard_map/all_gather | solution.py:125
  9.7 155.2 %all-gather.9.cloned.1.call-start = ((), (), s32[]{:S(2)}) async-start(), calls=%async_computation.4 | async-start | bytes 3342336 | tf_op jit(solution)/shard_map/all_gather | solution.py:131
  12.1 68.7 %copy-start.10 = (s32[8]{0:T(128)S(1)}, s32[8]{0:T(128)}, u32[]{:S(2)}) copy-start(s32[8]{0:T(128)} %param.23) | copy-start | bytes 100
  18.3 25.2 %all-to-all-start = ((bf16[128,2,1024]{2,1,0:T(2,128)(2,1)}), bf16[128,2,1024]{2,1,0:T(2,128)(2,1)S(1)}, u32[]{:S(2)}, u32[]{:S(2)}) async-start(bf16[128,2,1024]{2,1,0:T(2,128)(2,1)} %reshape.449), calls=%async_computation | async-start | bytes 1048576 | tf_op jit(solution)/shard_map/all_to_all | solution.py:77
  29.8 135.1 %all-gather.11.cloned.1.call-start = ((), (), s32[]{:S(2)}) async-start(), calls=%async_computation.5 | async-start | bytes 3342336 | tf_op jit(solution)/shard_map/all_gather | solution.py:137
  45.3 7.2 %collective-permute-start = (bf16[128,2048]{1,0:T(8,128)(2,1)S(1)}, bf16[128,2048]{1,0:T(8,128)(2,1)S(1)}, u32[]{:S(2)}, u32[]{:S(2)}) collective-permute-start(bf16[128,2048]{1,0:T(8,128)(2,1)S(1)} %gather_fusion.1), channel_id=1, source_target_pairs={{0,1},{1,2},{2,3},{3,4},{4,5},{5,6},{6,7},{7,0},{8,9},{9,10},{10,1... | collective-permute-start | bytes 1572872 | tf_op jit(solution)/shard_map/ppermute | solution.py:117
  52.4 8.6 %collective-permute-start.1 = (bf16[128,2048]{1,0:T(8,128)(2,1)S(1)}, bf16[128,2048]{1,0:T(8,128)(2,1)S(1)}, u32[]{:S(2)}, u32[]{:S(2)}) collective-permute-start(bf16[128,2048]{1,0:T(8,128)(2,1)S(1)} %collective-permute-done), channel_id=1, source_target_pairs={{0,1},{1,2},{2,3},{3,4},{4,5},{5,6},{6,7},{7,0},{8,9},{9,10},{10,1... | collective-permute-start | bytes 1572872 | tf_op jit(solution)/shard_map/ppermute | solution.py:117
  61.1 8.6 %collective-permute-start.2 = (bf16[128,2048]{1,0:T(8,128)(2,1)S(1)}, bf16[128,2048]{1,0:T(8,128)(2,1)S(1)}, u32[]{:S(2)}, u32[]{:S(2)}) collective-permute-start(bf16[128,2048]{1,0:T(8,128)(2,1)S(1)} %collective-permute-done.1), channel_id=1, source_target_pairs={{0,1},{1,2},{2,3},{3,4},{4,5},{5,6},{6,7},{7,0},{8,9},{9,10},{10,1... | collective-permute-start | bytes 1572872 | tf_op jit(solution)/shard_map/ppermute | solution.py:117
  69.7 8.6 %collective-permute-start.3 = (bf16[128,2048]{1,0:T(8,128)(2,1)S(1)}, bf16[128,2048]{1,0:T(8,128)(2,1)S(1)}, u32[]{:S(2)}, u32[]{:S(2)}) collective-permute-start(bf16[128,2048]{1,0:T(8,128)(2,1)S(1)} %collective-permute-done.2), channel_id=1, source_target_pairs={{0,1},{1,2},{2,3},{3,4},{4,5},{5,6},{6,7},{7,0},{8,9},{9,10},{10,1... | collective-permute-start | bytes 1572872 | tf_op jit(solution)/shard_map/ppermute | solution.py:117
  73.8 126.9 %all-gather.13.cloned.1.call-start = ((), (), s32[]{:S(2)}) async-start(), calls=%async_computation.6 | async-start | bytes 4718592 | tf_op jit(solution)/shard_map/all_gather | solution.py:187
  78.3 8.6 %collective-permute-start.4 = (bf16[128,2048]{1,0:T(8,128)(2,1)S(1)}, bf16[128,2048]{1,0:T(8,128)(2,1)S(1)}, u32[]{:S(2)}, u32[]{:S(2)}) collective-permute-start(bf16[128,2048]{1,0:T(8,128)(2,1)S(1)} %collective-permute-done.3), channel_id=1, source_target_pairs={{0,1},{1,2},{2,3},{3,4},{4,5},{5,6},{6,7},{7,0},{8,9},{9,10},{10,1... | collective-permute-start | bytes 1572872 | tf_op jit(solution)/shard_map/ppermute | solution.py:117
  86.9 9.9 %collective-permute-start.5 = (bf16[128,2048]{1,0:T(8,128)(2,1)S(1)}, bf16[128,2048]{1,0:T(8,128)(2,1)}, u32[]{:S(2)}, u32[]{:S(2)}) collective-permute-start(bf16[128,2048]{1,0:T(8,128)(2,1)S(1)} %collective-permute-done.4), channel_id=1, source_target_pairs={{0,1},{1,2},{2,3},{3,4},{4,5},{5,6},{6,7},{7,0},{8,9},{9,10},{10,1... | collective-permute-start | bytes 1572872 | tf_op jit(solution)/shard_map/ppermute | solution.py:117
  96.8 10.1 %collective-permute-start.6 = (bf16[128,2048]{1,0:T(8,128)(2,1)}, bf16[128,2048]{1,0:T(8,128)(2,1)}, u32[]{:S(2)}, u32[]{:S(2)}) collective-permute-start(bf16[128,2048]{1,0:T(8,128)(2,1)} %collective-permute-done.5), channel_id=1, source_target_pairs={{0,1},{1,2},{2,3},{3,4},{4,5},{5,6},{6,7},{7,0},{8,9},{9,10},{10,1... | collective-permute-start | bytes 1572872 | tf_op jit(solution)/shard_map/ppermute | solution.py:117
  109.2 3.6 copy-start.8
  111.6 4.1 copy-start.13
  111.8 6.2 %copy-start.3 = (bf16[2048,2048]{1,0:T(8,128)(2,1)}, bf16[2048,2048]{1,0:T(8,128)(2,1)S(1)}, u32[]{:S(2)}) copy-start(bf16[2048,2048]{1,0:T(8,128)(2,1)S(1)} %constant_dynamic-update-slice_fusion) | copy-start | bytes 25165828
  113.8 1.9 copy-start.2
  115.7 4.0 copy-start.6
  115.7 7.7 %copy-start.11 = (f32[128]{0:T(128)S(1)}, f32[128]{0:T(128)}, u32[]{:S(2)}) copy-start(f32[128]{0:T(128)} %param.34) | copy-start | bytes 1540
  115.7 9.2 %copy-start.12 = (f32[128]{0:T(128)S(1)}, f32[128]{0:T(128)}, u32[]{:S(2)}) copy-start(f32[128]{0:T(128)} %param.33) | copy-start | bytes 1540
  118.1 7.2 %copy-start.4 = (f32[1024,64]{1,0:T(8,128)S(1)}, f32[1024,64]{1,0:T(8,128)}, u32[]{:S(2)}) copy-start(f32[1024,64]{1,0:T(8,128)} %get-tuple-element.16) | copy-start | bytes 786436
  118.1 7.2 %copy-start.5 = (f32[1024,64]{1,0:T(8,128)S(1)}, f32[1024,64]{1,0:T(8,128)}, u32[]{:S(2)}) copy-start(f32[1024,64]{1,0:T(8,128)} %get-tuple-element.17) | copy-start | bytes 786436
  126.0 10.9 %copy-start.14 = (bf16[1,2048,128]{2,1,0:T(8,128)(2,1)S(1)}, bf16[1,2048,128]{2,1,0:T(8,128)(2,1)}, u32[]{:S(2)}) copy-start(bf16[1,2048,128]{2,1,0:T(8,128)(2,1)} %param.27) | copy-start | bytes 1572868
  136.8 16.0 %copy-start.15 = (bf16[1,2048,128]{2,1,0:T(8,128)(2,1)S(1)}, bf16[1,2048,128]{2,1,0:T(8,128)(2,1)}, u32[]{:S(2)}) copy-start(bf16[1,2048,128]{2,1,0:T(8,128)(2,1)} %param.28) | copy-start | bytes 1572868
  166.0 85.9 %all-gather.15.cloned.1.call-start = ((), (), s32[]{:S(2)}) async-start(), calls=%async_computation.7 | async-start | bytes 9437184 | tf_op jit(solution)/shard_map/all_gather | solution.py:122
  166.5 101.5 %copy-start.16 = (f32[2048]{0:T(1024)S(1)}, f32[2048]{0:T(1024)}, u32[]{:S(2)}) copy-start(f32[2048]{0:T(1024)} %param.36) | copy-start | bytes 24580
  166.6 181.3 %all-reduce.2.cloned.1.call-start = ((), (), s32[]{:S(2)}) async-start(), calls=%async_computation.9 | async-start | bytes 262144 | tf_op jit(solution)/shard_map/psum | solution.py:202
  266.1 2.0 copy-start.7
  289.2 59.7 %copy-start.9 = (f32[2048]{0:T(1024)S(1)}, f32[2048]{0:T(1024)}, u32[]{:S(2)}) copy-start(f32[2048]{0:T(1024)} %param.40) | copy-start | bytes 24580
  290.8 112.6 %reduce-scatter.2.cloned.1.call-start = ((), (), s32[]{:S(2)}) async-start(), calls=%async_computation.8 | async-start | bytes 9437184 | tf_op jit(solution)/shard_map/reduce_scatter | solution.py:196
  348.9 167.0 %copy-start.1 = (bf16[2048,384]{1,0:T(8,128)(2,1)S(1)}, bf16[2048,384]{1,0:T(8,128)(2,1)}, u32[]{:S(2)}) copy-start(bf16[2048,384]{1,0:T(8,128)(2,1)} %param.37) | copy-start | bytes 4718596
  408.2 104.8 %all-to-all-start.1 = ((bf16[128,2,1024]{2,1,0:T(2,128)(2,1)}), bf16[128,2,1024]{2,1,0:T(2,128)(2,1)S(1)}, u32[]{:S(2)}, u32[]{:S(2)}) async-start(bf16[128,2,1024]{2,1,0:T(2,128)(2,1)} %reshape.451), calls=%async_computation.2 | async-start | bytes 1048576 | tf_op jit(solution)/shard_map/all_to_all | solution.py:77
  (1 other events, 1.4 us)
Sparse Core Ops, SparseCore 0:
  10.2 55.7 all-gather.6
  68.0 46.8 all-gather.8
  117.1 46.9 all-gather.10
  166.2 34.3 all-gather.12
  202.2 49.6 all-gather.14
  291.0 56.8 all-reduce.1
  350.4 52.9 reduce-scatter.1
